TPU v7x, 256 devices: a whole 4x4x8 slice. The times are simulated.
256 devices in a mesh: space: 32 (over x, z), col: 8 (over y, core).
Axes of the slice: x: 4, y: 4, z: 8, core: 2. Of those that a mesh axis runs over, the one named last changes fastest.
Arguments:
- blocks: bfloat16 [2560, 24, 128, 128], P('space', 'col'), may hold values from -0.109375 to 0.109375
- basis_tiles: bfloat16 [2560, 128, 128], P('space'), may hold values from -6 to 6
- weights: float32 [2560, 128], P('space'), may hold values from 0.1 to 1
- neighbour_device: int32 [2560, 24], P('space', 'col'), may hold values from 0 to 31, as said below
- neighbour_row: int32 [2560, 24], P('space', 'col'), may hold values from 0 to 79
- counts: int32 [2560], P('space'), may hold values from 12 to 24
- aggregate: int32 [2560], P('space'), may hold values from 0 to 9
- pair_slot: int32 [2560, 24], P('space', 'col'), may hold values from 0 to 3
Outputs:
- coarse: float32 [1280, 128, 128], P(('space', 'col'))
Inputs may be any that keep to these rules, and one draw needn't show every extreme that they name: `neighbour_device`: among the slots of one device's 80 rows that fall to one index of col, exactly 60 name another device; no other device is named more than 3 times there, and some other device exactly 3 times.
All inputs are finite; a program needn't handle non-finite values.
Results may differ from a plain program's by a relative error of at most 0.0045.
Values may be sent and summed in bfloat16 or wider, within the bound.
A program may use at most 128 MiB of HBM per device.

v0:
```python
import jax
import jax.numpy as jnp
from jax import lax
from jax.sharding import PartitionSpec as P

KC = 4
CAP = 3
NCD = 10


def per_device(
    blocks, basis_tiles, weights, neighbour_device, neighbour_row, counts, aggregate, pair_slot
):
    space_count = lax.axis_size("space")
    own_index = lax.axis_index("space")
    col_index = lax.axis_index("col")
    row_count, slot_count = neighbour_device.shape
    block_size = blocks.shape[2]
    coarse_size = basis_tiles.shape[2]
    slot_total = row_count * slot_count
    peer_of = neighbour_device.reshape(slot_total)
    row_of = neighbour_row.reshape(slot_total)
    remote = peer_of != own_index
    onehot = (
        (peer_of[:, None] == jnp.arange(space_count, dtype=jnp.int32)[None, :]) & remote[:, None]
    ).astype(jnp.int32)
    position = jnp.sum((jnp.cumsum(onehot, axis=0) - onehot) * onehot, axis=1)
    bucket = jnp.where(remote, peer_of * CAP + position, space_count * CAP)
    requests = jnp.zeros((space_count * CAP,), jnp.int32).at[bucket].set(row_of, mode="drop")
    requests = requests.reshape(space_count, CAP)
    asked_rows = lax.all_to_all(requests, "space", split_axis=0, concat_axis=0, tiled=True)
    tile_index = jnp.where(remote, row_count + bucket, row_of)
    received = lax.all_to_all(
        basis_tiles[asked_rows], "space", split_axis=0, concat_axis=0, tiled=True
    )
    tile_table = jnp.concatenate(
        [basis_tiles, received.reshape(space_count * CAP, block_size, coarse_size)], axis=0
    )
    fetched = tile_table[tile_index].reshape(row_count, slot_count, block_size, coarse_size)
    slot_number = col_index * slot_count + jnp.arange(slot_count, dtype=jnp.int32)
    usable = slot_number[None, :] < counts[:, None]
    masked = jnp.where(usable[:, :, None, None], blocks, jnp.zeros((), blocks.dtype))
    partial_sum = jnp.einsum("rkab,rkbc->rac", masked, fetched, preferred_element_type=jnp.float32)
    smoothed = lax.psum(partial_sum, "col")
    prolong = (basis_tiles.astype(jnp.float32) - weights[:, :, None] * smoothed).astype(
        jnp.bfloat16
    )
    received_prolong = lax.all_to_all(
        prolong[asked_rows], "space", split_axis=0, concat_axis=0, tiled=True
    )
    prolong_table = jnp.concatenate(
        [prolong, received_prolong.reshape(space_count * CAP, block_size, coarse_size)], axis=0
    )
    neighbour_prolong = prolong_table[tile_index].reshape(
        row_count, slot_count, block_size, coarse_size
    )
    applied = jnp.einsum(
        "rkab,rkbc->rkac", masked, neighbour_prolong, preferred_element_type=jnp.float32
    ).astype(jnp.bfloat16)
    contribution = jnp.einsum(
        "rad,rkae->rkde", prolong, applied, preferred_element_type=jnp.float32
    )
    targets = (aggregate[:, None] * KC + pair_slot).reshape(slot_total)
    coarse_local = jax.ops.segment_sum(
        contribution.reshape(slot_total, coarse_size, coarse_size), targets, num_segments=NCD * KC
    )
    return lax.psum_scatter(coarse_local, "col", scatter_dimension=0, tiled=True)


def solution(mesh):
    return jax.shard_map(
        per_device,
        mesh=mesh,
        in_specs=(
            P("space", "col", None, None),
            P("space", None, None),
            P("space", None),
            P("space", "col"),
            P("space", "col"),
            P("space"),
            P("space"),
            P("space", "col"),
        ),
        out_specs=P(("space", "col"), None, None),
        check_vma=False,
    )
```

profile of v0, /device:TPU:6, one launch (start us, length us, event | category | flops | bytes accessed | tf_op | source)
XLA Modules:
  0.0 429.7 jit_solution(17318623963266410459)
XLA Ops:
  6.5 0.8 copy.26
  7.3 0.7 broadcast_multiply_fusion
  8.0 0.8 copy.29
  9.2 0.7 broadcast_compare_fusion.1
  11.5 1.3 scatter_custom_fusion
  12.9 19.3 %all_to_all.22 = s32[32,1,3]{2,1,0:T(1,128)S(1)} all-to-all(s32[32,1,3]{2,1,0:T(1,128)S(1)} %bitcast.44), channel_id=1, replica_groups=mesh['space'=32,'col'=8] {'space'}, dimensions={0} | all-to-all | bytes 768 | tf_op jit(solution)/shard_map/all_to_all | solution.py:31
  32.6 4.6 %gather_fusion = bf16[96,128,128]{2,1,0:T(8,128)(2,1)} fusion(bf16[80,128,128]{2,1,0:T(8,128)(2,1)} %param.9, s32[1024]{0:T(1024)S(1)} %pad_clamp_fusion.1), kind=kCustom, calls=%fused_computation | custom fusion | bytes 6291840 | tf_op jit(solution)/shard_map/gather | solution.py:34
  37.2 6.6 %all-to-all-start.1 = ((bf16[32,3,128,128]{3,2,1,0:T(8,128)(2,1)}), bf16[32,3,128,128]{3,2,1,0:T(8,128)(2,1)}, u32[]{:S(2)}, u32[]{:S(2)}) async-start(bf16[32,3,128,128]{3,2,1,0:T(8,128)(2,1)} %bitcast.41), calls=%async_computation.1 | async-start | bytes 6291456 | tf_op jit(solution)/shard_map/all_to_all | solution.py:33
  44.0 71.3 %all-to-all-done.1 = bf16[32,3,128,128]{3,2,1,0:T(8,128)(2,1)} async-done(((bf16[32,3,128,128]{3,2,1,0:T(8,128)(2,1)}), bf16[32,3,128,128]{3,2,1,0:T(8,128)(2,1)}, u32[]{:S(2)}, u32[]{:S(2)}) %all-to-all-start.1) | async-done | bytes 3145760 | tf_op jit(solution)/shard_map/all_to_all | solution.py:33
  115.3 4.9 %pad_maximum_fusion = bf16[176,128,128]{2,1,0:T(8,128)(2,1)} fusion(bf16[96,128,128]{2,1,0:T(8,128)(2,1)} %bitcast.6, bf16[80,128,128]{2,1,0:T(8,128)(2,1)S(1)} %copy-done.1), kind=kLoop, calls=%fused_computation.11 | loop fusion | flops 2883584 | bytes 11534336 | tf_op jit(solution)/shard_map/concatenate | solution.py:36
  120.2 11.1 %gather_fusion.1 = bf16[240,128,128]{2,1,0:T(8,128)(2,1)} fusion(bf16[176,128,128]{2,1,0:T(8,128)(2,1)} %pad_maximum_fusion, s32[1024]{0:T(1024)S(1)} %pad_clamp_fusion), kind=kCustom, calls=%fused_computation.1 | custom fusion | bytes 15729600 | tf_op jit(solution)/shard_map/gather | solution.py:39
  131.4 10.1 %fusion.8 = f32[80,128,128]{2,1,0:T(8,128)} fusion(bf16[80,3,128,128]{3,2,1,0:T(8,128)(2,1)} %bitcast.43, bf16[80,3,128,128]{3,2,1,0:T(8,128)(2,1)} %param.8, pred[80,3]{1,0:T(8,128)(4,1)S(1)} %broadcast_compare_fusion), kind=kOutput, calls=%fused_computation.17 | convolution fusion | flops 1010565120 | bytes 20971760 | tf_op jit(solution)/shard_map/rkab,rkbc->rac/dot_general | solution.py:43
  141.4 79.2 %all-reduce.3.cloned.1.call-done = f32[80,128,128]{2,1,0:T(8,128)} async-done(((f32[80,128,128]{2,1,0:T(8,128)}), f32[80,128,128]{2,1,0:T(8,128)}) %all-reduce.3.cloned.1.call-update) | async-done | bytes 5242896 | tf_op jit(solution)/shard_map/psum | solution.py:44
  220.7 4.6 %subtract_convert_fusion = bf16[80,128,128]{2,1,0:T(8,128)(2,1)S(1)} fusion(f32[80,128,128]{2,1,0:T(8,128)} %all-reduce.3.cloned.1.call-done, bf16[80,128,128]{2,1,0:T(8,128)(2,1)} %param.9, f32[80,128]{1,0:T(8,128)S(1)} %copy-done.2), kind=kLoop, calls=%fused_computation.13 | loop fusion | flops 5242880 | bytes 10526720 | tf_op jit(solution)/shard_map/convert_element_type | solution.py:45
  225.3 2.7 gather_fusion.2
  228.0 10.2 %all-to-all-start.2 = ((bf16[32,3,128,128]{3,2,1,0:T(8,128)(2,1)}), bf16[32,3,128,128]{3,2,1,0:T(8,128)(2,1)}, u32[]{:S(2)}, u32[]{:S(2)}) async-start(bf16[32,3,128,128]{3,2,1,0:T(8,128)(2,1)} %bitcast.42), calls=%async_computation.2 | async-start | bytes 6291456 | tf_op jit(solution)/shard_map/all_to_all | solution.py:48
  238.8 71.7 %all-to-all-done.2 = bf16[32,3,128,128]{3,2,1,0:T(8,128)(2,1)} async-done(((bf16[32,3,128,128]{3,2,1,0:T(8,128)(2,1)}), bf16[32,3,128,128]{3,2,1,0:T(8,128)(2,1)}, u32[]{:S(2)}, u32[]{:S(2)}) %all-to-all-start.2) | async-done | bytes 3145760 | tf_op jit(solution)/shard_map/all_to_all | solution.py:48
  310.5 4.9 %pad_maximum_fusion.1 = bf16[176,128,128]{2,1,0:T(8,128)(2,1)} fusion(bf16[96,128,128]{2,1,0:T(8,128)(2,1)} %bitcast.12, bf16[80,128,128]{2,1,0:T(8,128)(2,1)S(1)} %subtract_convert_fusion), kind=kLoop, calls=%fused_computation.12 | loop fusion | flops 2883584 | bytes 11534336 | tf_op jit(solution)/shard_map/concatenate | solution.py:51
  315.4 11.1 %gather_fusion.3 = bf16[240,128,128]{2,1,0:T(8,128)(2,1)} fusion(bf16[176,128,128]{2,1,0:T(8,128)(2,1)} %pad_maximum_fusion.1, s32[1024]{0:T(1024)S(1)} %pad_clamp_fusion), kind=kCustom, calls=%fused_computation.3 | custom fusion | bytes 15729600 | tf_op jit(solution)/shard_map/gather | solution.py:54
  326.5 11.1 %fusion = f32[80,3,128,128]{3,2,1,0:T(8,128)} fusion(bf16[80,3,128,128]{3,2,1,0:T(8,128)(2,1)} %bitcast.40, bf16[80,3,128,128]{3,2,1,0:T(8,128)(2,1)} %param.8, pred[80,3]{1,0:T(8,128)(4,1)S(1)} %broadcast_compare_fusion, bf16[80,128,128]{2,1,0:T(8,128)(2,1)S(1)} %subtract_convert_fusion), kind=kOutput, calls=%fused_computation.6 | convolution fusion | flops 2021130240 | bytes 34078960 | tf_op jit(solution)/shard_map/rad,rkae->rkde/dot_general | solution.py:60
  337.6 15.7 %copy.35 = f32[240,128,128]{2,1,0:T(8,128)} copy(f32[240,128,128]{1,2,0:T(8,128)} %bitcast.39) | data formatting | bytes 31457280 | tf_op jit(solution)/shard_map/reshape | solution.py:65
  353.6 31.5 %scatter_fusion = f32[40,128,128]{2,1,0:T(8,128)S(1)} fusion(f32[40,128,128]{2,1,0:T(8,128)S(1)} %broadcast_in_dim.20, s32[240]{0:T(256)S(1)} %reshape.230, f32[240,128,128]{2,1,0:T(8,128)} %copy.35), kind=kCustom, calls=%fused_computation.5 | custom fusion | flops 3932160 | bytes 47186880 | tf_op jit(solution)/shard_map/scatter-add | solution.py:64
  385.1 1.5 copy-done
  386.7 36.2 %reduce-scatter.2.cloned.1.call-done = f32[5,128,128]{2,1,0:T(8,128)} async-done(((f32[40,128,128]{2,1,0:T(8,128)}), f32[5,128,128]{2,1,0:T(8,128)}) %reduce-scatter.2.cloned.1.call-update) | async-done | bytes 327696 | tf_op jit(solution)/shard_map/reduce_scatter | solution.py:67
  (46 shorter events, 3.3 us)
Async XLA Ops:
  32.6 11.4 %copy-start.4 = (s32[80]{0:T(128)S(1)}, s32[80]{0:T(128)}, u32[]{:S(2)}) copy-start(s32[80]{0:T(128)} %param.13) | copy-start | bytes 964
  32.6 82.7 %copy-start.1 = (bf16[80,128,128]{2,1,0:T(8,128)(2,1)S(1)}, bf16[80,128,128]{2,1,0:T(8,128)(2,1)}, u32[]{:S(2)}) copy-start(bf16[80,128,128]{2,1,0:T(8,128)(2,1)} %param.9) | copy-start | bytes 7864324
  37.2 78.1 %all-to-all-start.1 = ((bf16[32,3,128,128]{3,2,1,0:T(8,128)(2,1)}), bf16[32,3,128,128]{3,2,1,0:T(8,128)(2,1)}, u32[]{:S(2)}, u32[]{:S(2)}) async-start(bf16[32,3,128,128]{3,2,1,0:T(8,128)(2,1)} %bitcast.41), calls=%async_computation.1 | async-start | bytes 6291456 | tf_op jit(solution)/shard_map/all_to_all | solution.py:33
  43.9 176.8 %all-reduce.3.cloned.1.call-start = ((), (), s32[]{:S(2)}) async-start(), calls=%async_computation.4 | async-start | bytes 10485760 | tf_op jit(solution)/shard_map/psum | solution.py:44
  131.4 89.3 %copy-start.2 = (f32[80,128]{1,0:T(8,128)S(1)}, f32[80,128]{1,0:T(8,128)}, u32[]{:S(2)}) copy-start(f32[80,128]{1,0:T(8,128)} %param.10) | copy-start | bytes 122884
  225.3 13.2 %copy-start.5 = (s32[80]{0:T(128)S(1)}, s32[80]{0:T(128)}, u32[]{:S(2)}) copy-start(s32[80]{0:T(128)} %param.14) | copy-start | bytes 964
  225.3 13.2 %copy-start.3 = (s32[80,3]{0,1:T(4,128)S(1)}, s32[80,3]{0,1:T(4,128)}, u32[]{:S(2)}) copy-start(s32[80,3]{0,1:T(4,128)} %param.15) | copy-start | bytes 2884
  228.0 82.5 %all-to-all-start.2 = ((bf16[32,3,128,128]{3,2,1,0:T(8,128)(2,1)}), bf16[32,3,128,128]{3,2,1,0:T(8,128)(2,1)}, u32[]{:S(2)}, u32[]{:S(2)}) async-start(bf16[32,3,128,128]{3,2,1,0:T(8,128)(2,1)} %bitcast.42), calls=%async_computation.2 | async-start | bytes 6291456 | tf_op jit(solution)/shard_map/all_to_all | solution.py:48
  238.3 184.5 %reduce-scatter.2.cloned.1.call-start = ((), (), s32[]{:S(2)}) async-start(), calls=%async_computation.5 | async-start | bytes 2949120 | tf_op jit(solution)/shard_map/reduce_scatter | solution.py:67
  385.1 1.5 copy-start
Sparse Core Ops, SparseCore 0:
  141.6 79.0 all-reduce.2
  386.8 35.9 reduce-scatter.1
where the time goes:
time: 431 us; the launch traced here: 430 us
  waiting for transfers between devices  258 us (60%)
  local copies, waits for them, and re-layouts  51.8 us (12%)
  other arithmetic  48.2 us (11%)
  matrix products  21.2 us (5%)
  blocking collectives  19.3 us (4%)
  starting transfers between devices  17.1 us (4%)
  between operations  13.6 us (3%)
    psum x1, waiting for transfers between devices, per_device(): smoothed = lax.psum(partial_sum, 'col')  79.2 us
    all_to_all x1, waiting for transfers between devices, per_device(): lax.all_to_all(prolong[asked_rows], 'space', split_axis=0, concat_axis=0,...  71.7 us
    all_to_all x1, waiting for transfers between devices, per_device(): lax.all_to_all(basis_tiles[asked_rows], 'space', split_axis=0, concat_axi...  71.3 us
    reduce_scatter x1, waiting for transfers between devices, per_device(): lax.psum_scatter(coarse_local, 'col', scatter_dimension=0, tiled=True)  36.2 us
    scatter-add x1, other arithmetic, per_device(): jax.ops.segment_sum(contribution.reshape(slot_total, coarse_size, coarse_...  31.5 us
    all_to_all x1, blocking collectives, per_device(): lax.all_to_all(requests, 'space', split_axis=0, concat_axis=0, tiled=True)  19.3 us
    reshape x1, local copies, waits for them, and re-layouts, per_device(): contribution.reshape(slot_total, coarse_size, coarse_size)  15.7 us
    gather x1, local copies, waits for them, and re-layouts, per_device(): prolong_table[tile_index]  11.1 us
  transfers between devices with their start and end apart: 4, of which 4 were waited for; matrix products, arithmetic and copies ran while one was open for 0% of the time, Pallas kernels for 0%

commit v1 on v0

--- a/solution.py
+++ b/solution.py
@@ -41,7 +41,9 @@
     usable = slot_number[None, :] < counts[:, None]
     masked = jnp.where(usable[:, :, None, None], blocks, jnp.zeros((), blocks.dtype))
     partial_sum = jnp.einsum("rkab,rkbc->rac", masked, fetched, preferred_element_type=jnp.float32)
-    smoothed = lax.psum(partial_sum, "col")
+    smoothed = partial_sum
+    for hop in (1, 2, 4):
+        smoothed = smoothed + lax.ppermute(smoothed, "col", [(dev, dev ^ hop) for dev in range(8)])
     prolong = (basis_tiles.astype(jnp.float32) - weights[:, :, None] * smoothed).astype(
         jnp.bfloat16
     )

time: 431 us -> 584 us (1.35)
  waiting for transfers between devices: 258 us -> 412 us
    ppermute x0 -> x3, waiting for transfers between devices: none -> 235 us  [per_device(): lax.ppermute(smoothed, 'col', [(dev, dev ^ hop) for dev in range(8)])]
    psum x1 -> x0, waiting for transfers between devices: 79.2 us -> none  [per_device(): smoothed = lax.psum(partial_sum, 'col')]
  transfers between devices with their start and end apart: 4 -> 6, of which waited for: 4 -> 6; matrix products, arithmetic and copies ran while one was open for 0% -> 0% of each run, Pallas kernels for 0% -> 0%
where the time goes in v1:
time: 584 us; the launch traced here: 583 us
  waiting for transfers between devices  412 us (71%)
  local copies, waits for them, and re-layouts  51.8 us (9%)
  other arithmetic  48.4 us (8%)
  blocking collectives  19.3 us (3%)
  matrix products  18.8 us (3%)
  starting transfers between devices  18.7 us (3%)
  between operations  13.7 us (2%)
    ppermute x3, waiting for transfers between devices, per_device(): lax.ppermute(smoothed, 'col', [(dev, dev ^ hop) for dev in range(8)])  235 us
    all_to_all x1, waiting for transfers between devices, per_device(): lax.all_to_all(basis_tiles[asked_rows], 'space', split_axis=0, concat_axi...  71.3 us
    all_to_all x1, waiting for transfers between devices, per_device(): lax.all_to_all(prolong[asked_rows], 'space', split_axis=0, concat_axis=0,...  71.1 us
    reduce_scatter x1, waiting for transfers between devices, per_device(): lax.psum_scatter(coarse_local, 'col', scatter_dimension=0, tiled=True)  35.2 us
    scatter-add x1, other arithmetic, per_device(): jax.ops.segment_sum(contribution.reshape(slot_total, coarse_size, coarse_...  31.5 us
    all_to_all x1, blocking collectives, per_device(): lax.all_to_all(requests, 'space', split_axis=0, concat_axis=0, tiled=True)  19.3 us
    reshape x1, local copies, waits for them, and re-layouts, per_device(): contribution.reshape(slot_total, coarse_size, coarse_size)  15.7 us
  transfers between devices with their start and end apart: 6, of which 6 were waited for; matrix products, arithmetic and copies ran while one was open for 0% of the time, Pallas kernels for 0%

profile of v1, /device:TPU:6, one launch (start us, length us, event | category | flops | bytes accessed | tf_op | source)
XLA Modules:
  0.0 583.1 jit_solution(3059425702327754791)
XLA Ops:
  12.9 19.3 %all_to_all.22 = s32[32,1,3]{2,1,0:T(1,128)S(1)} all-to-all(s32[32,1,3]{2,1,0:T(1,128)S(1)} %bitcast.44), channel_id=1, replica_groups=mesh['space'=32,'col'=8] {'space'}, dimensions={0} | all-to-all | bytes 768 | tf_op jit(solution)/shard_map/all_to_all | solution.py:31
  32.6 4.6 gather_fusion
  37.2 6.6 %all-to-all-start.1 = ((bf16[32,3,128,128]{3,2,1,0:T(8,128)(2,1)}), bf16[32,3,128,128]{3,2,1,0:T(8,128)(2,1)}, u32[]{:S(2)}, u32[]{:S(2)}) async-start(bf16[32,3,128,128]{3,2,1,0:T(8,128)(2,1)} %bitcast.41), calls=%async_computation.1 | async-start | bytes 6291456 | tf_op jit(solution)/shard_map/all_to_all | solution.py:33
  44.0 71.3 %all-to-all-done.1 = bf16[32,3,128,128]{3,2,1,0:T(8,128)(2,1)} async-done(((bf16[32,3,128,128]{3,2,1,0:T(8,128)(2,1)}), bf16[32,3,128,128]{3,2,1,0:T(8,128)(2,1)}, u32[]{:S(2)}, u32[]{:S(2)}) %all-to-all-start.1) | async-done | bytes 3145760 | tf_op jit(solution)/shard_map/all_to_all | solution.py:33
  115.3 4.9 pad_maximum_fusion
  120.2 11.1 %gather_fusion.1 = bf16[240,128,128]{2,1,0:T(8,128)(2,1)} fusion(bf16[176,128,128]{2,1,0:T(8,128)(2,1)} %pad_maximum_fusion, s32[1024]{0:T(1024)S(1)} %pad_clamp_fusion), kind=kCustom, calls=%fused_computation.1 | custom fusion | bytes 15729600 | tf_op jit(solution)/shard_map/gather | solution.py:39
  131.4 7.7 %fusion.8 = f32[80,128,128]{2,1,0:T(8,128)S(1)} fusion(bf16[80,3,128,128]{3,2,1,0:T(8,128)(2,1)} %bitcast.43, bf16[80,3,128,128]{3,2,1,0:T(8,128)(2,1)} %param.8, pred[80,3]{1,0:T(8,128)(4,1)S(1)} %broadcast_compare_fusion), kind=kOutput, calls=%fused_computation.17 | convolution fusion | flops 1010565120 | bytes 20971760 | tf_op jit(solution)/shard_map/rkab,rkbc->rac/dot_general | solution.py:43
  139.2 8.6 %collective-permute-done = f32[80,128,128]{2,1,0:T(8,128)S(1)} collective-permute-done((f32[80,128,128]{2,1,0:T(8,128)S(1)}, f32[80,128,128]{2,1,0:T(8,128)S(1)}, u32[]{:S(2)}, u32[]{:S(2)}) %collective-permute-start) | collective-permute-done | bytes 5242912 | tf_op jit(solution)/shard_map/ppermute | solution.py:46
  149.4 1.8 collective-permute-start.1
  151.2 113.5 %collective-permute-done.1 = f32[80,128,128]{2,1,0:T(8,128)S(1)} collective-permute-done((f32[80,128,128]{2,1,0:T(8,128)S(1)}, f32[80,128,128]{2,1,0:T(8,128)S(1)}, u32[]{:S(2)}, u32[]{:S(2)}) %collective-permute-start.1) | collective-permute-done | bytes 5242912 | tf_op jit(solution)/shard_map/ppermute | solution.py:46
  264.7 1.5 add.102
  266.2 3.3 collective-permute-start.2
  269.5 112.5 %collective-permute-done.2 = f32[80,128,128]{2,1,0:T(8,128)S(1)} collective-permute-done((f32[80,128,128]{2,1,0:T(8,128)S(1)}, f32[80,128,128]{2,1,0:T(8,128)S(1)}, u32[]{:S(2)}, u32[]{:S(2)}) %collective-permute-start.2) | collective-permute-done | bytes 5242912 | tf_op jit(solution)/shard_map/ppermute | solution.py:46
  382.0 1.9 subtract_convert_fusion
  383.9 2.7 gather_fusion.2
  386.6 6.8 %all-to-all-start.2 = ((bf16[32,3,128,128]{3,2,1,0:T(8,128)(2,1)}), bf16[32,3,128,128]{3,2,1,0:T(8,128)(2,1)}, u32[]{:S(2)}, u32[]{:S(2)}) async-start(bf16[32,3,128,128]{3,2,1,0:T(8,128)(2,1)} %bitcast.42), calls=%async_computation.2 | async-start | bytes 6291456 | tf_op jit(solution)/shard_map/all_to_all | solution.py:50
  393.8 71.1 %all-to-all-done.2 = bf16[32,3,128,128]{3,2,1,0:T(8,128)(2,1)} async-done(((bf16[32,3,128,128]{3,2,1,0:T(8,128)(2,1)}), bf16[32,3,128,128]{3,2,1,0:T(8,128)(2,1)}, u32[]{:S(2)}, u32[]{:S(2)}) %all-to-all-start.2) | async-done | bytes 3145760 | tf_op jit(solution)/shard_map/all_to_all | solution.py:50
  464.9 4.9 pad_maximum_fusion.1
  469.8 11.1 %gather_fusion.3 = bf16[240,128,128]{2,1,0:T(8,128)(2,1)} fusion(bf16[176,128,128]{2,1,0:T(8,128)(2,1)} %pad_maximum_fusion.1, s32[1024]{0:T(1024)S(1)} %pad_clamp_fusion), kind=kCustom, calls=%fused_computation.3 | custom fusion | bytes 15729600 | tf_op jit(solution)/shard_map/gather | solution.py:56
  480.9 11.1 %fusion = f32[80,3,128,128]{3,2,1,0:T(8,128)} fusion(bf16[80,3,128,128]{3,2,1,0:T(8,128)(2,1)} %bitcast.40, bf16[80,3,128,128]{3,2,1,0:T(8,128)(2,1)} %param.8, pred[80,3]{1,0:T(8,128)(4,1)S(1)} %broadcast_compare_fusion, bf16[80,128,128]{2,1,0:T(8,128)(2,1)S(1)} %subtract_convert_fusion), kind=kOutput, calls=%fused_computation.6 | convolution fusion | flops 2021130240 | bytes 34078960 | tf_op jit(solution)/shard_map/rad,rkae->rkde/dot_general | solution.py:62
  492.0 15.7 %copy.35 = f32[240,128,128]{2,1,0:T(8,128)} copy(f32[240,128,128]{1,2,0:T(8,128)} %bitcast.39) | data formatting | bytes 31457280 | tf_op jit(solution)/shard_map/reshape | solution.py:67
  508.0 31.5 %scatter_fusion = f32[40,128,128]{2,1,0:T(8,128)S(1)} fusion(f32[40,128,128]{2,1,0:T(8,128)S(1)} %broadcast_in_dim.20, s32[240]{0:T(256)S(1)} %reshape.230, f32[240,128,128]{2,1,0:T(8,128)} %copy.35), kind=kCustom, calls=%fused_computation.5 | custom fusion | flops 3932160 | bytes 47186880 | tf_op jit(solution)/shard_map/scatter-add | solution.py:66
  539.5 1.5 copy-done
  541.1 35.2 %reduce-scatter.2.cloned.1.call-done = f32[5,128,128]{2,1,0:T(8,128)} async-done(((f32[40,128,128]{2,1,0:T(8,128)}), f32[5,128,128]{2,1,0:T(8,128)}) %reduce-scatter.2.cloned.1.call-update) | async-done | bytes 327696 | tf_op jit(solution)/shard_map/reduce_scatter | solution.py:69
  (53 shorter events, 8.9 us)
Async XLA Ops:
  32.6 11.3 %copy-start.5 = (s32[80]{0:T(128)S(1)}, s32[80]{0:T(128)}, u32[]{:S(2)}) copy-start(s32[80]{0:T(128)} %param.13) | copy-start | bytes 964
  32.6 82.7 %copy-start.1 = (bf16[80,128,128]{2,1,0:T(8,128)(2,1)S(1)}, bf16[80,128,128]{2,1,0:T(8,128)(2,1)}, u32[]{:S(2)}) copy-start(bf16[80,128,128]{2,1,0:T(8,128)(2,1)} %param.9) | copy-start | bytes 7864324
  37.2 78.1 %all-to-all-start.1 = ((bf16[32,3,128,128]{3,2,1,0:T(8,128)(2,1)}), bf16[32,3,128,128]{3,2,1,0:T(8,128)(2,1)}, u32[]{:S(2)}, u32[]{:S(2)}) async-start(bf16[32,3,128,128]{3,2,1,0:T(8,128)(2,1)} %bitcast.41), calls=%async_computation.1 | async-start | bytes 6291456 | tf_op jit(solution)/shard_map/all_to_all | solution.py:33
  139.1 8.7 %collective-permute-start = (f32[80,128,128]{2,1,0:T(8,128)S(1)}, f32[80,128,128]{2,1,0:T(8,128)S(1)}, u32[]{:S(2)}, u32[]{:S(2)}) collective-permute-start(f32[80,128,128]{2,1,0:T(8,128)S(1)} %fusion.8), channel_id=1, source_target_pairs={{0,1},{1,0},{2,3},{3,2},{4,5},{5,4},{6,7},{7,6},{8,9},{9,8},{10,11... | collective-permute-start | bytes 15728648 | tf_op jit(solution)/shard_map/ppermute | solution.py:46
  149.3 232.7 %copy-start.2 = (bf16[80,128,128]{2,1,0:T(8,128)(2,1)S(1)}, bf16[80,128,128]{2,1,0:T(8,128)(2,1)}, u32[]{:S(2)}) copy-start(bf16[80,128,128]{2,1,0:T(8,128)(2,1)} %param.9) | copy-start | bytes 7864324
  149.4 232.7 %copy-start.3 = (f32[80,128]{1,0:T(8,128)S(1)}, f32[80,128]{1,0:T(8,128)}, u32[]{:S(2)}) copy-start(f32[80,128]{1,0:T(8,128)} %param.10) | copy-start | bytes 122884
  149.4 115.4 %collective-permute-start.1 = (f32[80,128,128]{2,1,0:T(8,128)S(1)}, f32[80,128,128]{2,1,0:T(8,128)S(1)}, u32[]{:S(2)}, u32[]{:S(2)}) collective-permute-start(f32[80,128,128]{2,1,0:T(8,128)S(1)} %add.101), channel_id=1, source_target_pairs={{0,2},{1,3},{2,0},{3,1},{4,6},{5,7},{6,4},{7,5},{8,10},{9,11},{10,... | collective-permute-start | bytes 15728648 | tf_op jit(solution)/shard_map/ppermute | solution.py:46
  266.2 115.8 %collective-permute-start.2 = (f32[80,128,128]{2,1,0:T(8,128)S(1)}, f32[80,128,128]{2,1,0:T(8,128)S(1)}, u32[]{:S(2)}, u32[]{:S(2)}) collective-permute-start(f32[80,128,128]{2,1,0:T(8,128)S(1)} %add.102), channel_id=1, source_target_pairs={{0,4},{1,5},{2,6},{3,7},{4,0},{5,1},{6,2},{7,3},{8,12},{9,13},{10,... | collective-permute-start | bytes 15728648 | tf_op jit(solution)/shard_map/ppermute | solution.py:46
  383.9 9.6 %copy-start.6 = (s32[80]{0:T(128)S(1)}, s32[80]{0:T(128)}, u32[]{:S(2)}) copy-start(s32[80]{0:T(128)} %param.14) | copy-start | bytes 964
  383.9 9.6 %copy-start.4 = (s32[80,3]{0,1:T(4,128)S(1)}, s32[80,3]{0,1:T(4,128)}, u32[]{:S(2)}) copy-start(s32[80,3]{0,1:T(4,128)} %param.15) | copy-start | bytes 2884
  386.6 78.3 %all-to-all-start.2 = ((bf16[32,3,128,128]{3,2,1,0:T(8,128)(2,1)}), bf16[32,3,128,128]{3,2,1,0:T(8,128)(2,1)}, u32[]{:S(2)}, u32[]{:S(2)}) async-start(bf16[32,3,128,128]{3,2,1,0:T(8,128)(2,1)} %bitcast.42), calls=%async_computation.2 | async-start | bytes 6291456 | tf_op jit(solution)/shard_map/all_to_all | solution.py:50
  393.5 182.7 %reduce-scatter.2.cloned.1.call-start = ((), (), s32[]{:S(2)}) async-start(), calls=%async_computation.4 | async-start | bytes 2949120 | tf_op jit(solution)/shard_map/reduce_scatter | solution.py:69
  539.5 1.5 copy-start
Sparse Core Ops, SparseCore 0:
  541.2 34.9 reduce-scatter.1
